TPU v7x, 32 devices: a whole 2x2x4 slice. The times are simulated.
32 devices in a mesh: groups: 1, ctx: 32 (over z, y, x, core).
Axes of the slice: x: 2, y: 2, z: 4, core: 2. Of those that a mesh axis runs over, the one named last changes fastest.
Arguments:
- prefill_query: bfloat16 [1024, 32, 576], P('groups', 'ctx'), may hold values from -1000 to 1000
- prefill_latent: bfloat16 [1024, 576], P(('groups', 'ctx')), may hold values from -6 to 6
- decode_query: bfloat16 [2, 32, 576], P('groups'), may hold values from -1000 to 1000
- cache: bfloat16 [2, 16384, 576], P('groups', 'ctx'), may hold values from -6 to 6
- lengths: int32 [2], P('groups'), may hold values from 2049 to 16384
- page_table: int32 [64, 2], P('groups'), may hold values from 0 to 31, as said below
Outputs:
- prefill_out: bfloat16 [1024, 32, 512], P('groups', 'ctx')
- decode_out: bfloat16 [2, 32, 512], P('groups', 'ctx')
Inputs may be any that keep to these rules, and one draw needn't show every extreme that they name: `page_table`: row p names the device (column 0, below 32) and the pool slot (column 1, below 16) that take latent page p; no two rows name the same pair.
All inputs are finite; a program needn't handle non-finite values.
Results may differ from a plain program's by a relative error of at most 0.0049.
Values may be sent and summed in bfloat16 or wider, within the bound.
No kernel may reach another device: no remote copies, remote signals or barrier semaphores. Data moves between devices by JAX's collectives and lax.ppermute only.
A program may use at most 64 MiB of HBM per device.

v0:
```python
import jax
import jax.numpy as jnp
from jax import lax
from jax.sharding import PartitionSpec as P

D_LAT = 512
PAGE = 16
POOL = 16
REQ = 2
SCALE = 192.0 ** (-0.5)
NEG = -1e30


def attend_block(state_now, queries, shard_rows, first_row):
    run_max, run_sum, weighted = state_now
    length = shard_rows.shape[0]
    scores = (
        jnp.einsum("ihc,jc->ihj", queries, shard_rows, preferred_element_type=jnp.float32) * SCALE
    )
    row_index = jnp.arange(queries.shape[0], dtype=jnp.int32)
    key_index = first_row + jnp.arange(length, dtype=jnp.int32)
    allowed = (key_index[None, :] <= row_index[:, None])[:, None, :]
    masked = jnp.where(allowed, scores, NEG)
    new_max = jnp.maximum(run_max, jnp.max(masked, axis=2))
    weights = jnp.where(allowed, jnp.exp(scores - new_max[:, :, None]), 0.0)
    factor = jnp.exp(run_max - new_max)
    new_sum = run_sum * factor + jnp.sum(weights, axis=2)
    product = jnp.einsum(
        "ihj,jv->ihv",
        weights.astype(jnp.bfloat16),
        shard_rows[:, :D_LAT],
        preferred_element_type=jnp.float32,
    )
    return (new_max, new_sum, weighted * factor[:, :, None] + product)


def attend_blocks(state_now, queries, shard_rows, first_row):
    length = shard_rows.shape[0]
    block_rows = min(length, 512)
    starts = list(range(0, length, block_rows))
    for start in starts:
        stop = min(start + block_rows, length)
        state_now = attend_block(state_now, queries, shard_rows[start:stop], first_row + start)
    return state_now


def pick_rows(shard_rows, first_row, source_rows, pool_live):
    length = shard_rows.shape[0]
    local_rows = source_rows - first_row
    inside = (local_rows >= 0) & (local_rows < length) & pool_live
    taken = jnp.take(shard_rows, jnp.clip(local_rows, 0, length - 1), axis=0)
    return jnp.where(inside[:, None], taken, jnp.zeros_like(taken))


def shards(prefill_query, prefill_latent, decode_query, cache, lengths, page_table):
    device = lax.axis_index("ctx")
    span = prefill_query.shape[0]
    head_here = prefill_query.shape[1]
    width = prefill_latent.shape[1]
    page_count = page_table.shape[0]
    slot_index = jnp.arange(POOL, dtype=jnp.int32)
    chosen = (page_table[None, :, 0] == device) & (page_table[None, :, 1] == slot_index[:, None])
    slot_live = jnp.any(chosen, axis=1)
    slot_page = jnp.sum(
        jnp.where(chosen, jnp.arange(page_count, dtype=jnp.int32)[None, :], 0), axis=1
    )
    offsets = jnp.arange(PAGE, dtype=jnp.int32)
    source_rows = (slot_page[:, None] * PAGE + offsets[None, :]).reshape(-1)
    pool_live = jnp.repeat(slot_live, PAGE)
    pool_request = jnp.repeat((device * POOL + slot_index) % REQ, PAGE)
    initial = (
        jnp.full((span, head_here), NEG, jnp.float32),
        jnp.zeros((span, head_here), jnp.float32),
        jnp.zeros((span, head_here, D_LAT), jnp.float32),
        jnp.zeros((POOL * PAGE, width), jnp.bfloat16),
    )
    gathered = lax.all_gather(prefill_latent, "ctx", axis=0, tiled=True)
    attended = attend_blocks(initial[:3], prefill_query, gathered, 0)
    final = attended + (pick_rows(gathered, 0, source_rows, pool_live),)
    run_max, run_sum, weighted, pool_rows = final
    prefill_out = (weighted / run_sum[:, :, None]).astype(jnp.bfloat16)
    cache_dev = cache.shape[1]
    positions = device * cache_dev + jnp.arange(cache_dev, dtype=jnp.int32)
    resident_ok = (positions[None, :] < lengths[:, None])[:, None, :]
    resident_scores = (
        jnp.einsum("rhc,rtc->rht", decode_query, cache, preferred_element_type=jnp.float32) * SCALE
    )
    request_index = jnp.arange(REQ, dtype=jnp.int32)
    pool_ok = ((pool_request[None, :] == request_index[:, None]) & pool_live[None, :])[:, None, :]
    pool_scores = (
        jnp.einsum("rhc,kc->rhk", decode_query, pool_rows, preferred_element_type=jnp.float32)
        * SCALE
    )
    part_max = jnp.maximum(
        jnp.max(jnp.where(resident_ok, resident_scores, NEG), axis=2),
        jnp.max(jnp.where(pool_ok, pool_scores, NEG), axis=2),
    )
    resident_weights = jnp.where(resident_ok, jnp.exp(resident_scores - part_max[:, :, None]), 0.0)
    pool_weights = jnp.where(pool_ok, jnp.exp(pool_scores - part_max[:, :, None]), 0.0)
    part_sum = jnp.sum(resident_weights, axis=2) + jnp.sum(pool_weights, axis=2)
    part_out = jnp.einsum(
        "rht,rtv->rhv",
        resident_weights.astype(jnp.bfloat16),
        cache[:, :, :D_LAT],
        preferred_element_type=jnp.float32,
    )
    part_out = part_out + jnp.einsum(
        "rhk,kv->rhv",
        pool_weights.astype(jnp.bfloat16),
        pool_rows[:, :D_LAT],
        preferred_element_type=jnp.float32,
    )
    moved_max, moved_sum, moved_out = (
        lax.all_to_all(part_max[None], "ctx", split_axis=2, concat_axis=0, tiled=True),
        lax.all_to_all(part_sum[None], "ctx", split_axis=2, concat_axis=0, tiled=True),
        lax.all_to_all(part_out[None], "ctx", split_axis=2, concat_axis=0, tiled=True),
    )
    top_all = jnp.max(moved_max, axis=0)
    scales = jnp.exp(moved_max - top_all[None])
    own_sum = jnp.sum(moved_sum * scales, axis=0)
    own_out = jnp.sum(moved_out * scales[..., None], axis=0)
    decode_out = (own_out / own_sum[:, :, None]).astype(jnp.bfloat16)
    return (prefill_out, decode_out)


def solution(mesh):
    in_specs = (
        P("groups", "ctx", None),
        P(("groups", "ctx"), None),
        P("groups", None, None),
        P("groups", "ctx", None),
        P("groups"),
        P("groups", None),
    )
    out_specs = (P("groups", "ctx", None), P("groups", "ctx", None))
    return jax.shard_map(shards, mesh=mesh, in_specs=in_specs, out_specs=out_specs, check_vma=False)
```

profile of v0, /device:TPU:0, one launch (start us, length us, event | category | flops | bytes accessed | tf_op | source)
XLA Modules:
  0.0 114.0 jit_solution(10159602554596118152)
XLA Ops:
  7.2 0.7 all-gather.2.cloned.1.call-update
  7.9 0.7 slice_bitcast_fusion.2
  8.6 0.7 compare_bitcast_fusion
  9.3 0.1 select_reduce_fusion.4
  9.8 0.1 fusion.45
  10.4 0.7 broadcast_compare_fusion
  11.1 1.7 %select_reduce_fusion.2 = (f32[2,32]{1,0:T(2,128)S(1)}, f32[2,32,512]{2,1,0:T(8,128)S(1)}) fusion(pred[2,512]{1,0:T(4,128)(4,1)S(1)} %broadcast_compare_fusion, bf16[2,32,576]{2,1,0:T(8,128)(2,1)} %param.8, bf16[2,512,576]{1,2,0:T(8,128)(2,1)} %param.9), kind=kOutput, calls=%fused_computation.42 | convolution fusion | flops 37846976 | bytes 1385728 | tf_op jit(solution)/shard_map/rhc,rtc->rht/dot_general | solution.py:86
  12.8 55.0 %all-gather.2.cloned.1.call-done = bf16[1024,576]{1,0:T(8,128)(2,1)} async-done(((bf16[32,576]{1,0:T(8,128)(2,1)}), bf16[1024,576]{1,0:T(8,128)(2,1)}) %all-gather.2.cloned.1.call-update) | async-done | bytes 1179664 | tf_op jit(solution)/shard_map/all_gather | solution.py:77
  67.9 2.9 %gather_fusion = bf16[256,576]{1,0:T(8,128)(2,1)S(1)} fusion(bf16[1024,576]{1,0:T(8,128)(2,1)} %all-gather.2.cloned.1.call-done, s32[1024]{0:T(1024)S(1)} %pad_clamp_fusion), kind=kCustom, calls=%fused_computation | custom fusion | bytes 590848 | tf_op jit(solution)/shard_map/jit(_take)/gather | solution.py:51
  70.8 0.2 select_select_fusion
  70.9 0.3 select_reduce_fusion.3
  71.2 0.2 fusion.27
  71.5 0.2 fusion.35
  71.6 0.7 copy.21
  72.3 3.5 %all-to-all-start.1 = ((f32[1,2,32]{1,0,2:T(1,128)}), f32[1,2,32]{1,0,2:T(1,128)S(1)}, u32[]{:S(2)}, u32[]{:S(2)}) async-start(f32[1,2,32]{1,0,2:T(1,128)} %copy.21), calls=%async_computation.1 | async-start | bytes 32768 | tf_op jit(solution)/shard_map/all_to_all | solution.py:114
  75.8 0.2 fusion.29
  76.0 1.0 select_reduce_fusion.1
  77.0 1.0 select_reduce_fusion
  78.1 0.9 fusion
  79.0 0.8 fusion.12
  79.7 2.1 %fusion.4 = bf16[1024,1,512]{2,0,1:T(8,128)(2,1)} fusion(f32[1024,512]{1,0:T(8,128)S(1)} %fusion.12, f32[1024,512]{0,1:T(8,128)S(1)} %get-tuple-element.10, f32[1024]{0:T(1024)S(1)} %get-tuple-element.2, f32[1024]{0:T(1024)S(1)} %get-tuple-element.5, f32[1024]{0:T(1024)S(1)} %get-tuple-element.3, s32[512]{0:T(512)S(1)} %iota_add_fusion.2, ...), kind=kOutput, calls=%fused_computation.12 | convolution fusion | flops 542113792 | bytes 5785600 | tf_op jit(solution)/shard_map/ihj,jv->ihv/dot_general | solution.py:28
  81.9 0.7 copy.24
  82.5 0.5 all-to-all-done.1
  83.0 5.4 %all-to-all-start.2 = ((f32[1,2,32]{1,0,2:T(1,128)}), f32[1,2,32]{1,0,2:T(1,128)S(1)}, u32[]{:S(2)}, u32[]{:S(2)}) async-start(f32[1,2,32]{1,0,2:T(1,128)} %copy.24), calls=%async_computation.2 | async-start | bytes 32768 | tf_op jit(solution)/shard_map/all_to_all | solution.py:115
  88.4 1.6 %fusion.9 = f32[1,2,32,512]{3,2,1,0:T(8,128)S(1)} fusion(f32[2,32,512]{2,1,0:T(8,128)S(1)} %fusion.27, bf16[2,512,576]{1,2,0:T(8,128)(2,1)} %param.9, f32[2,32,512]{2,1,0:T(8,128)S(1)} %get-tuple-element.12, f32[2,32]{1,0:T(2,128)S(1)} %max.39, pred[2,512]{1,0:T(4,128)(4,1)S(1)} %broadcast_compare_fusion), kind=kOutput, calls=%fused_computation.18 | convolution fusion | flops 33685504 | bytes 1443072 | tf_op jit(solution)/shard_map/rht,rtv->rhv/dot_general | solution.py:101
  90.0 0.8 copy.20
  90.9 4.7 %all-to-all-done.2 = f32[1,2,32]{1,0,2:T(1,128)S(1)} async-done(((f32[1,2,32]{1,0,2:T(1,128)}), f32[1,2,32]{1,0,2:T(1,128)S(1)}, u32[]{:S(2)}, u32[]{:S(2)}) %all-to-all-start.2) | async-done | bytes 288 | tf_op jit(solution)/shard_map/all_to_all | solution.py:115
  95.6 2.6 %all-to-all-start = ((f32[1,2,32,512]{3,1,0,2:T(2,128)}), f32[1,2,32,512]{3,1,0,2:T(2,128)S(1)}, u32[]{:S(2)}, u32[]{:S(2)}) async-start(f32[1,2,32,512]{3,1,0,2:T(2,128)} %copy.20), calls=%async_computation | async-start | bytes 262144 | tf_op jit(solution)/shard_map/all_to_all | solution.py:116
  98.4 0.2 fusion.50
  98.6 7.8 %all-to-all-done = f32[1,2,32,512]{3,1,0,2:T(2,128)S(1)} async-done(((f32[1,2,32,512]{3,1,0,2:T(2,128)}), f32[1,2,32,512]{3,1,0,2:T(2,128)S(1)}, u32[]{:S(2)}, u32[]{:S(2)}) %all-to-all-start) | async-done | bytes 131104 | tf_op jit(solution)/shard_map/all_to_all | solution.py:116
  106.3 0.1 fusion.28
  106.5 0.7 fusion.47
  (34 shorter events, 1.2 us)
Async XLA Ops:
  7.2 68.8 %copy-start = (bf16[1024,1,576]{0,2,1:T(8,128)(2,1)S(1)}, bf16[1024,1,576]{0,2,1:T(8,128)(2,1)}, u32[]{:S(2)}) copy-start(bf16[1024,1,576]{0,2,1:T(8,128)(2,1)} %param.6) | copy-start | bytes 3538948
  7.2 60.7 %all-gather.2.cloned.1.call-start = ((), (), s32[]{:S(2)}) async-start(), calls=%async_computation.3 | async-start | bytes 1351680 | tf_op jit(solution)/shard_map/all_gather | solution.py:77
  12.8 58.1 %copy-start.2 = (bf16[2,32,576]{2,1,0:T(8,128)(2,1)S(1)}, bf16[2,32,576]{2,1,0:T(8,128)(2,1)}, u32[]{:S(2)}) copy-start(bf16[2,32,576]{2,1,0:T(8,128)(2,1)} %param.8) | copy-start | bytes 221188
  67.9 8.1 %copy-start.1 = (bf16[1024,576]{1,0:T(8,128)(2,1)S(1)}, bf16[1024,576]{1,0:T(8,128)(2,1)}, u32[]{:S(2)}) copy-start(bf16[1024,576]{1,0:T(8,128)(2,1)} %all-gather.2.cloned.1.call-done) | copy-start | bytes 3538948
  72.3 10.7 %all-to-all-start.1 = ((f32[1,2,32]{1,0,2:T(1,128)}), f32[1,2,32]{1,0,2:T(1,128)S(1)}, u32[]{:S(2)}, u32[]{:S(2)}) async-start(f32[1,2,32]{1,0,2:T(1,128)} %copy.21), calls=%async_computation.1 | async-start | bytes 32768 | tf_op jit(solution)/shard_map/all_to_all | solution.py:114
  83.0 12.6 %all-to-all-start.2 = ((f32[1,2,32]{1,0,2:T(1,128)}), f32[1,2,32]{1,0,2:T(1,128)S(1)}, u32[]{:S(2)}, u32[]{:S(2)}) async-start(f32[1,2,32]{1,0,2:T(1,128)} %copy.24), calls=%async_computation.2 | async-start | bytes 32768 | tf_op jit(solution)/shard_map/all_to_all | solution.py:115
  95.6 10.8 %all-to-all-start = ((f32[1,2,32,512]{3,1,0,2:T(2,128)}), f32[1,2,32,512]{3,1,0,2:T(2,128)S(1)}, u32[]{:S(2)}, u32[]{:S(2)}) async-start(f32[1,2,32,512]{3,1,0,2:T(2,128)} %copy.20), calls=%async_computation | async-start | bytes 262144 | tf_op jit(solution)/shard_map/all_to_all | solution.py:116
Sparse Core Ops, SparseCore 0:
  10.8 56.9 all-gather.1
where the time goes:
time: 114 us
  waiting for transfers between devices  68.6 us (60%)
  between operations  14.2 us (12%)
  starting transfers between devices  11.5 us (10%)
  matrix products  8.79 us (8%)
  local copies, waits for them, and re-layouts  6.53 us (6%)
  other arithmetic  4.38 us (4%)
    all_gather x1, waiting for transfers between devices, shards(): gathered = lax.all_gather(prefill_latent, 'ctx', axis=0, tiled=True)  55 us
    all_to_all x1, waiting for transfers between devices, shards(): lax.all_to_all(part_out[None], 'ctx', split_axis=2, concat_axis=0, tiled=...  7.77 us
    all_to_all x1, starting transfers between devices, shards(): lax.all_to_all(part_sum[None], 'ctx', split_axis=2, concat_axis=0, tiled=...  5.38 us
    all_to_all x1, waiting for transfers between devices, shards(): lax.all_to_all(part_sum[None], 'ctx', split_axis=2, concat_axis=0, tiled=...  4.65 us
    all_to_all x1, starting transfers between devices, shards(): lax.all_to_all(part_max[None], 'ctx', split_axis=2, concat_axis=0, tiled=...  3.48 us
    gather x1, local copies, waits for them, and re-layouts, pick_rows(): taken = jnp.take(shard_rows, jnp.clip(local_rows, 0, length - 1), axis=0)  2.89 us
    dot_general x2, matrix products, attend_block(): jnp.einsum('ihj,jv->ihv', weights.astype(jnp.bfloat16), shard_rows[:, :D_...  2.87 us
    all_to_all x1, starting transfers between devices, shards(): lax.all_to_all(part_out[None], 'ctx', split_axis=2, concat_axis=0, tiled=...  2.57 us
  transfers between devices with their start and end apart: 4, of which 4 were waited for; matrix products, arithmetic and copies ran while one was open for 13% of the time, Pallas kernels for 0%

commit v1 on v0

--- a/solution.py
+++ b/solution.py
@@ -9,6 +9,13 @@
 REQ = 2
 SCALE = 192.0 ** (-0.5)
 NEG = -1e30
+
+
+def trade_parts(shard, name, split, join):
+    peers = lax.axis_size(name)
+    blocks = jnp.stack(jnp.split(shard, peers, axis=split), axis=0)
+    blocks = lax.all_to_all(blocks, name, split_axis=0, concat_axis=0)
+    return jnp.concatenate(blocks, axis=join)
 
 
 def attend_block(state_now, queries, shard_rows, first_row):
@@ -112,7 +119,7 @@
     )
     moved_max, moved_sum, moved_out = (
         lax.all_to_all(part_max[None], "ctx", split_axis=2, concat_axis=0, tiled=True),
-        lax.all_to_all(part_sum[None], "ctx", split_axis=2, concat_axis=0, tiled=True),
+        trade_parts(part_sum[None], "ctx", 2, 0),
         lax.all_to_all(part_out[None], "ctx", split_axis=2, concat_axis=0, tiled=True),
     )
     top_all = jnp.max(moved_max, axis=0)

time: 114 us -> 132 us (1.16)
  local copies, waits for them, and re-layouts: 6.53 us -> 24.2 us
    unnamed x6 -> x37, local copies, waits for them, and re-layouts: 0.02 us -> 16.9 us
  transfers between devices with their start and end apart: 4 -> 4, of which waited for: 4 -> 3; matrix products, arithmetic and copies ran while one was open for 13% -> 23% of each run, Pallas kernels for 0% -> 0%
where the time goes in v1:
time: 132 us
  waiting for transfers between devices  68.1 us (52%)
  local copies, waits for them, and re-layouts  24.2 us (18%)
  between operations  14.2 us (11%)
  starting transfers between devices  11.9 us (9%)
  matrix products  8.77 us (7%)
  other arithmetic  4.38 us (3%)
    all_gather x1, waiting for transfers between devices, shards(): gathered = lax.all_gather(prefill_latent, 'ctx', axis=0, tiled=True)  55 us
    unnamed x37, local copies, waits for them, and re-layouts  16.9 us
    all_to_all x1, waiting for transfers between devices, shards(): lax.all_to_all(part_out[None], 'ctx', split_axis=2, concat_axis=0, tiled=...  7.77 us
    all_to_all x1, starting transfers between devices, trade_parts(): blocks = lax.all_to_all(blocks, name, split_axis=0, concat_axis=0)  5.83 us
    all_to_all x1, waiting for transfers between devices, trade_parts(): blocks = lax.all_to_all(blocks, name, split_axis=0, concat_axis=0)  4.65 us
    all_to_all x1, starting transfers between devices, shards(): lax.all_to_all(part_max[None], 'ctx', split_axis=2, concat_axis=0, tiled=...  3.48 us
    gather x1, local copies, waits for them, and re-layouts, pick_rows(): taken = jnp.take(shard_rows, jnp.clip(local_rows, 0, length - 1), axis=0)  2.89 us
    dot_general x2, matrix products, attend_block(): jnp.einsum('ihj,jv->ihv', weights.astype(jnp.bfloat16), shard_rows[:, :D_...  2.86 us
  transfers between devices with their start and end apart: 4, of which 3 were waited for; matrix products, arithmetic and copies ran while one was open for 23% of the time, Pallas kernels for 0%

profile of v1, /device:TPU:0, one launch (start us, length us, event | category | flops | bytes accessed | tf_op | source)
XLA Modules:
  0.0 131.7 jit_solution(16980731557011177522)
XLA Ops:
  7.2 0.7 all-gather.2.cloned.1.call-update
  7.9 0.7 slice_bitcast_fusion.2
  8.6 0.7 compare_bitcast_fusion
  10.4 0.7 broadcast_compare_fusion
  11.1 1.7 %select_reduce_fusion.2 = (f32[2,32]{1,0:T(2,128)S(1)}, f32[2,32,512]{2,1,0:T(8,128)S(1)}) fusion(pred[2,512]{1,0:T(4,128)(4,1)S(1)} %broadcast_compare_fusion, bf16[2,32,576]{2,1,0:T(8,128)(2,1)} %param.8, bf16[2,512,576]{1,2,0:T(8,128)(2,1)} %param.9), kind=kOutput, calls=%fused_computation.42 | convolution fusion | flops 37846976 | bytes 1385728 | tf_op jit(solution)/shard_map/rhc,rtc->rht/dot_general | solution.py:93
  12.8 55.0 %all-gather.2.cloned.1.call-done = bf16[1024,576]{1,0:T(8,128)(2,1)} async-done(((bf16[32,576]{1,0:T(8,128)(2,1)}), bf16[1024,576]{1,0:T(8,128)(2,1)}) %all-gather.2.cloned.1.call-update) | async-done | bytes 1179664 | tf_op jit(solution)/shard_map/all_gather | solution.py:84
  67.9 2.9 %gather_fusion = bf16[256,576]{1,0:T(8,128)(2,1)S(1)} fusion(bf16[1024,576]{1,0:T(8,128)(2,1)} %all-gather.2.cloned.1.call-done, s32[1024]{0:T(1024)S(1)} %pad_clamp_fusion), kind=kCustom, calls=%fused_computation | custom fusion | bytes 590848 | tf_op jit(solution)/shard_map/jit(_take)/gather | solution.py:58
  73.3 0.7 copy.95
  74.0 3.5 %all-to-all-start.1 = ((f32[1,2,32]{1,0,2:T(1,128)}), f32[1,2,32]{1,0,2:T(1,128)S(1)}, u32[]{:S(2)}, u32[]{:S(2)}) async-start(f32[1,2,32]{1,0,2:T(1,128)} %copy.95), calls=%async_computation.1 | async-start | bytes 32768 | tf_op jit(solution)/shard_map/all_to_all | solution.py:121
  78.6 0.6 constant_dynamic-update-slice_fusion.28
  79.1 0.6 constant_dynamic-update-slice_fusion.27
  80.8 0.6 constant_dynamic-update-slice_fusion.24
  84.0 0.6 constant_dynamic-update-slice_fusion.18
  84.6 0.6 constant_dynamic-update-slice_fusion.17
  85.7 0.6 constant_dynamic-update-slice_fusion.15
  87.2 0.6 constant_dynamic-update-slice_fusion.12
  88.9 0.6 constant_dynamic-update-slice_fusion.9
  90.5 0.6 constant_dynamic-update-slice_fusion.6
  91.1 0.6 constant_dynamic-update-slice_fusion.5
  92.2 0.6 constant_dynamic-update-slice_fusion.3
  93.8 1.0 select_reduce_fusion.1
  94.8 1.0 select_reduce_fusion
  95.9 0.9 fusion
  96.8 0.8 fusion.12
  97.6 2.1 %fusion.4 = bf16[1024,1,512]{2,0,1:T(8,128)(2,1)} fusion(f32[1024,512]{1,0:T(8,128)S(1)} %fusion.12, f32[1024,512]{0,1:T(8,128)S(1)} %get-tuple-element.42, f32[1024]{0:T(1024)S(1)} %get-tuple-element.34, f32[1024]{0:T(1024)S(1)} %get-tuple-element.37, f32[1024]{0:T(1024)S(1)} %get-tuple-element.35, s32[512]{0:T(512)S(1)} %iota_add_fusion.2, ...), kind=kOutput, calls=%fused_computation.12 | convolution fusion | flops 542113792 | bytes 5785600 | tf_op jit(solution)/shard_map/ihj,jv->ihv/dot_general | solution.py:35
  100.2 5.8 %all-to-all-start.2 = ((f32[32,1,2,1]{2,3,1,0:T(1,128)}), f32[32,1,2,1]{2,3,1,0:T(1,128)S(1)}, u32[]{:S(2)}, u32[]{:S(2)}) async-start(f32[32,1,2,1]{2,3,1,0:T(1,128)} %constant_dynamic-update-slice_fusion), calls=%async_computation.2 | async-start | bytes 32768 | tf_op jit(solution)/shard_map/all_to_all | solution.py:17
  106.1 1.6 %fusion.9 = f32[1,2,32,512]{3,2,1,0:T(8,128)S(1)} fusion(f32[2,32,512]{2,1,0:T(8,128)S(1)} %fusion.27, bf16[2,512,576]{1,2,0:T(8,128)(2,1)} %param.9, f32[2,32,512]{2,1,0:T(8,128)S(1)} %get-tuple-element.44, f32[2,32]{1,0:T(2,128)S(1)} %max.39, pred[2,512]{1,0:T(4,128)(4,1)S(1)} %broadcast_compare_fusion), kind=kOutput, calls=%fused_computation.18 | convolution fusion | flops 33685504 | bytes 1443072 | tf_op jit(solution)/shard_map/rht,rtv->rhv/dot_general | solution.py:108
  107.7 0.8 copy.94
  108.6 4.7 %all-to-all-done.2 = f32[32,1,2,1]{2,3,1,0:T(1,128)S(1)} async-done(((f32[32,1,2,1]{2,3,1,0:T(1,128)}), f32[32,1,2,1]{2,3,1,0:T(1,128)S(1)}, u32[]{:S(2)}, u32[]{:S(2)}) %all-to-all-start.2) | async-done | bytes 288 | tf_op jit(solution)/shard_map/all_to_all | solution.py:17
  113.2 2.6 %all-to-all-start = ((f32[1,2,32,512]{3,1,0,2:T(2,128)}), f32[1,2,32,512]{3,1,0,2:T(2,128)S(1)}, u32[]{:S(2)}, u32[]{:S(2)}) async-start(f32[1,2,32,512]{3,1,0,2:T(2,128)} %copy.94), calls=%async_computation | async-start | bytes 262144 | tf_op jit(solution)/shard_map/all_to_all | solution.py:123
  116.3 7.8 %all-to-all-done = f32[1,2,32,512]{3,1,0,2:T(2,128)S(1)} async-done(((f32[1,2,32,512]{3,1,0,2:T(2,128)}), f32[1,2,32,512]{3,1,0,2:T(2,128)S(1)}, u32[]{:S(2)}, u32[]{:S(2)}) %all-to-all-start) | async-done | bytes 131104 | tf_op jit(solution)/shard_map/all_to_all | solution.py:123
  124.2 0.7 fusion.47
  (67 shorter events, 14.8 us)
Async XLA Ops:
  7.2 86.7 %copy-start = (bf16[1024,1,576]{0,2,1:T(8,128)(2,1)S(1)}, bf16[1024,1,576]{0,2,1:T(8,128)(2,1)}, u32[]{:S(2)}) copy-start(bf16[1024,1,576]{0,2,1:T(8,128)(2,1)} %param.6) | copy-start | bytes 3538948
  7.2 60.7 %all-gather.2.cloned.1.call-start = ((), (), s32[]{:S(2)}) async-start(), calls=%async_computation.3 | async-start | bytes 1351680 | tf_op jit(solution)/shard_map/all_gather | solution.py:84
  12.8 58.1 %copy-start.2 = (bf16[2,32,576]{2,1,0:T(8,128)(2,1)S(1)}, bf16[2,32,576]{2,1,0:T(8,128)(2,1)}, u32[]{:S(2)}) copy-start(bf16[2,32,576]{2,1,0:T(8,128)(2,1)} %param.8) | copy-start | bytes 221188
  67.9 26.0 %copy-start.1 = (bf16[1024,576]{1,0:T(8,128)(2,1)S(1)}, bf16[1024,576]{1,0:T(8,128)(2,1)}, u32[]{:S(2)}) copy-start(bf16[1024,576]{1,0:T(8,128)(2,1)} %all-gather.2.cloned.1.call-done) | copy-start | bytes 3538948
  74.0 26.3 %all-to-all-start.1 = ((f32[1,2,32]{1,0,2:T(1,128)}), f32[1,2,32]{1,0,2:T(1,128)S(1)}, u32[]{:S(2)}, u32[]{:S(2)}) async-start(f32[1,2,32]{1,0,2:T(1,128)} %copy.95), calls=%async_computation.1 | async-start | bytes 32768 | tf_op jit(solution)/shard_map/all_to_all | solution.py:121
  100.2 13.0 %all-to-all-start.2 = ((f32[32,1,2,1]{2,3,1,0:T(1,128)}), f32[32,1,2,1]{2,3,1,0:T(1,128)S(1)}, u32[]{:S(2)}, u32[]{:S(2)}) async-start(f32[32,1,2,1]{2,3,1,0:T(1,128)} %constant_dynamic-update-slice_fusion), calls=%async_computation.2 | async-start | bytes 32768 | tf_op jit(solution)/shard_map/all_to_all | solution.py:17
  113.2 10.8 %all-to-all-start = ((f32[1,2,32,512]{3,1,0,2:T(2,128)}), f32[1,2,32,512]{3,1,0,2:T(2,128)S(1)}, u32[]{:S(2)}, u32[]{:S(2)}) async-start(f32[1,2,32,512]{3,1,0,2:T(2,128)} %copy.94), calls=%async_computation | async-start | bytes 262144 | tf_op jit(solution)/shard_map/all_to_all | solution.py:123
Sparse Core Ops, SparseCore 0:
  10.8 56.9 all-gather.1
